TPU v7x, 512 devices: a whole 4x4x16 slice. The times are simulated.
512 devices in a mesh: row: 32 (over z, core), col: 16 (over x, y).
Axes of the slice: x: 4, y: 4, z: 16, core: 2. Of those that a mesh axis runs over, the one named last changes fastest.
Arguments:
- weight: bfloat16 [8192, 53248], P('row', 'col'), may hold values from -6 to 6
- inverse_rows: float32 [512, 53248], P('row', 'col'), as said below
- pruned_index: int32 [512], replicated, may hold values from 0 to 53247, as said below
Outputs:
- pruned_weight: bfloat16 [8192, 53248], P('row', 'col')
- saliency: float32 [8192], P('row')
Inputs may be any that keep to these rules, and one draw needn't show every extreme that they name: `pruned_index`: distinct and ascending. Neuron c lies in column shard c // 3328; at most 96 of them lie in one shard, and exactly 96 in one shard. `inverse_rows`: its columns pruned_index form a symmetric positive definite matrix.
All inputs are finite; a program needn't handle non-finite values.
Results may differ from a plain program's by a relative error of at most 0.001.
Values may be sent and summed in bfloat16 or wider, within the bound.
A program may use at most 64 MiB of HBM per device.

v0:
```python
import jax
import jax.numpy as jnp
from jax import lax
from jax.sharding import Mesh
from jax.sharding import PartitionSpec as P

ROW = ("row_0", "row_1")


def from_everyone(value, axis):
    count = lax.axis_size(axis)
    return lax.all_to_all(
        jnp.broadcast_to(value[None], (count, *value.shape)), axis, 0, 0, tiled=True
    )


def joined_along(parts, dim):
    parts = jnp.moveaxis(parts, 0, dim)
    shape = parts.shape
    return parts.reshape(*shape[:dim], shape[dim] * shape[dim + 1], *shape[dim + 2 :])


def gather_directly(value, axis, dim):
    parts = from_everyone(value, axis)
    return joined_along(parts, dim)


def all_blocks(value, axes, sequence):
    parts = value[None]
    for k in sequence:
        parts = lax.all_gather(parts, axes[k], axis=0, tiled=True)
    carried = [lax.axis_size(axes[k]) for k in reversed(sequence)]
    parts = parts.reshape(*carried, *value.shape)
    turned = sorted(range(len(sequence)), key=lambda place: sequence[len(sequence) - 1 - place])
    return parts.transpose(*turned, *range(len(sequence), parts.ndim)).reshape(-1, *value.shape)


def whole_of(value, axes, sequence, dim):
    return joined_along(all_blocks(value, axes, sequence), dim)


def body(weight, inverse_rows, pruned_index):
    row_count, col_width = weight.shape
    pruned_count = pruned_index.shape[0]
    col_devices = lax.axis_size("col")
    own_index = lax.axis_index("col")
    col_anchor = own_index * col_width
    capacity = 3 * pruned_count // col_devices
    boundary = jnp.arange(col_devices + 1, dtype=jnp.int32) * col_width
    edges_at = jnp.sum((pruned_index[None, :] < boundary[:, None]).astype(jnp.int32), axis=1)
    starts = edges_at[:-1]
    counts = edges_at[1:] - edges_at[:-1]
    window_start = starts[own_index]
    padded = jnp.concatenate([pruned_index, jnp.full((capacity,), -1, jnp.int32)])
    window = lax.dynamic_slice_in_dim(padded, window_start, capacity) - col_anchor
    slot_ids = jnp.arange(capacity, dtype=jnp.int32)
    occupied = slot_ids < counts[own_index]
    clipped = jnp.clip(window, 0, col_width - 1)
    column_ids = lax.broadcasted_iota(jnp.int32, (col_width, capacity), 0)
    picker = ((column_ids == clipped[None, :]) & occupied[None, :]).astype(jnp.bfloat16)
    weight_window = jnp.dot(weight, picker, preferred_element_type=jnp.float32).astype(jnp.bfloat16)
    inverse_window = jnp.where(occupied[None, :], jnp.take(inverse_rows, clipped, axis=1), 0.0)
    weight_all = gather_directly(weight_window, "col", 1)
    inverse_all = gather_directly(inverse_window, "col", 1)
    targets = (starts[:, None] + slot_ids[None, :]).reshape(-1)
    is_valid = (slot_ids[None, :] < counts[:, None]).reshape(-1)
    neuron_ids = lax.broadcasted_iota(jnp.int32, (col_devices * capacity, pruned_count), 1)
    placer = (neuron_ids == targets[:, None]) & is_valid[:, None]
    weight_pruned = jnp.dot(
        weight_all, placer.astype(jnp.bfloat16), preferred_element_type=jnp.float32
    )
    schur_part = jnp.dot(
        inverse_all,
        placer.astype(jnp.float32),
        precision=lax.Precision.HIGHEST,
        preferred_element_type=jnp.float32,
    )
    schur_block = whole_of(schur_part, ROW, (0, 1), 0)
    factor_low = jnp.linalg.cholesky(schur_block)
    solved = jax.scipy.linalg.cho_solve((factor_low, True), weight_pruned.T).T
    correction = jnp.dot(
        solved,
        lax.all_gather(inverse_rows, ROW, axis=0, tiled=True),
        precision=lax.Precision.HIGHEST,
        preferred_element_type=jnp.float32,
    )
    pruned_weight = (weight.astype(jnp.float32) - correction).astype(jnp.bfloat16)
    saliency = jnp.sum(solved * weight_pruned, axis=1) / (2.0 * pruned_count)
    return (pruned_weight, saliency)


def solution(mesh):
    split = Mesh(mesh.devices.reshape(16, 2, mesh.shape["col"]), ("row_0", "row_1", "col"))
    return jax.shard_map(
        body,
        mesh=split,
        in_specs=(P(ROW, "col"), P(ROW, "col"), P()),
        out_specs=(P(ROW, "col"), P(ROW)),
        check_vma=False,
    )
```

profile of v0, /device:TPU:8, one launch (start us, length us, event | category | flops | bytes accessed | tf_op | source)
XLA Modules:
  0.0 250.3 jit_solution(7870224598733661959)
XLA Ops:
  11.5 1.5 compare_and_fusion
  12.9 1.4 copy.33
  15.8 9.1 %all-to-all-start = ((f32[16,16,96]{2,1,0:T(8,128)}), f32[16,16,96]{2,1,0:T(8,128)S(1)}, u32[]{:S(2)}, u32[]{:S(2)}) async-start(f32[16,16,96]{2,1,0:T(8,128)} %broadcast_in_dim.56), calls=%async_computation | async-start | bytes 262144 | tf_op jit(solution)/shard_map/all_to_all | solution.py:12
  25.3 6.1 %all-to-all-done = f32[16,16,96]{2,1,0:T(8,128)S(1)} async-done(((f32[16,16,96]{2,1,0:T(8,128)}), f32[16,16,96]{2,1,0:T(8,128)S(1)}, u32[]{:S(2)}, u32[]{:S(2)}) %all-to-all-start) | async-done | bytes 98336 | tf_op jit(solution)/shard_map/all_to_all | solution.py:12
  31.6 1.2 fusion.4
  32.8 39.3 %all-gather = f32[256,512]{1,0:T(8,128)} all-gather(f32[16,512]{1,0:T(8,128)S(1)} %fusion.4), channel_id=2, replica_groups=mesh['row_0'=16,'row_1'=2,'col'=16] {'row_0'}, dimensions={0}, use_global_device_ids=true | all-gather | bytes 557056 | tf_op jit(solution)/shard_map/all_gather | solution.py:31
  74.5 5.5 %all-to-all-start.1 = ((bf16[16,256,96]{1,2,0:T(8,128)(2,1)}), bf16[16,256,96]{1,2,0:T(8,128)(2,1)S(1)}, u32[]{:S(2)}, u32[]{:S(2)}) async-start(bf16[16,256,96]{1,2,0:T(8,128)(2,1)} %broadcast_in_dim.58), calls=%async_computation.1 | async-start | bytes 1572864 | tf_op jit(solution)/shard_map/all_to_all | solution.py:12
  80.0 9.7 %all-to-all-done.1 = bf16[16,256,96]{1,2,0:T(8,128)(2,1)S(1)} async-done(((bf16[16,256,96]{1,2,0:T(8,128)(2,1)}), bf16[16,256,96]{1,2,0:T(8,128)(2,1)S(1)}, u32[]{:S(2)}, u32[]{:S(2)}) %all-to-all-start.1) | async-done | bytes 786464 | tf_op jit(solution)/shard_map/all_to_all | solution.py:12
  89.7 2.0 fusion.2
  91.7 1.3 copy.36
  93.6 11.7 %cholesky.104 = f32[128,128]{1,0:T(8,128)S(1)} custom-call(f32[128,128]{1,0:T(8,128)S(1)} %cholesky.266), custom_call_target="Cholesky" | custom-call | tf_op jit(solution)/shard_map/jit(cholesky)/cholesky | solution.py:79
  105.4 9.8 %custom-call.34 = f32[1,128,128]{1,2,0:T(8,128)S(1)} custom-call(f32[1,128,128]{2,1,0:T(8,128)S(1)} %get-tuple-element.31), custom_call_target="InvertDiagBlocksLowerTriangular" | custom-call | tf_op jit(solution)/shard_map/jit(cholesky)/cholesky | solution.py:79
  115.9 11.7 %cholesky.217 = f32[128,128]{1,0:T(8,128)S(1)} custom-call(f32[128,128]{1,0:T(8,128)S(1)} %cholesky.270), custom_call_target="Cholesky" | custom-call | tf_op jit(solution)/shard_map/jit(cholesky)/cholesky | solution.py:79
  127.7 10.0 %custom-call.35 = f32[1,128,128]{1,2,0:T(8,128)S(1)} custom-call(f32[1,128,128]{2,1,0:T(8,128)S(1)} %get-tuple-element.28), custom_call_target="InvertDiagBlocksLowerTriangular" | custom-call | tf_op jit(solution)/shard_map/jit(cholesky)/cholesky | solution.py:79
  138.3 11.7 %cholesky.238 = f32[128,128]{1,0:T(8,128)S(1)} custom-call(f32[128,128]{1,0:T(8,128)S(1)} %cholesky.275), custom_call_target="Cholesky" | custom-call | tf_op jit(solution)/shard_map/jit(cholesky)/cholesky | solution.py:79
  150.1 9.8 %custom-call.36 = f32[1,128,128]{1,2,0:T(8,128)S(1)} custom-call(f32[1,128,128]{2,1,0:T(8,128)S(1)} %get-tuple-element.25), custom_call_target="InvertDiagBlocksLowerTriangular" | custom-call | tf_op jit(solution)/shard_map/jit(cholesky)/cholesky | solution.py:79
  160.5 11.9 %cholesky.255 = f32[128,128]{1,0:T(8,128)S(1)} custom-call(f32[128,128]{1,0:T(8,128)S(1)} %convolution_subtract_fusion.9), custom_call_target="Cholesky" | custom-call | tf_op jit(solution)/shard_map/jit(cholesky)/cholesky | solution.py:79
  178.0 8.2 %while.1 = (s32[]{:T(128)}, f32[512,512]{1,0:T(8,128)S(1)}, s32[4,2]{0,1:T(2,128)S(1)}, f32[4,128,128]{2,1,0:T(8,128)S(1)}, s32[]{:T(128)}) while((s32[]{:T(128)}, f32[512,512]{1,0:T(8,128)S(1)}, s32[4,2]{0,1:T(2,128)S(1)}, f32[4,128,128]{2,1,0:T(8,128)S(1)}, s32[]{:T(128)}) %tuple.33), condition=%wide.while_cond, body=%wide.while_body.sunk | while | flops 2 | bytes 131181 | solution.py:80
  178.7 1.3 bitcast_dynamic-update-slice_fusion.2
  180.7 1.3 bitcast_dynamic-update-slice_fusion.2
  182.8 1.3 bitcast_dynamic-update-slice_fusion.2
  184.8 1.3 bitcast_dynamic-update-slice_fusion.2
  186.2 39.3 %custom-call.37 = f32[4,128,128]{1,2,0:T(8,128)S(1)} custom-call(f32[4,128,128]{2,1,0:T(8,128)S(1)} %get-tuple-element.9), custom_call_target="InvertDiagBlocksLowerTriangular" | custom-call | tf_op jit(solution)/shard_map/jit(_cho_solve)/triangular_solve | solution.py:80
  232.0 11.3 %fusion = bf16[256,3328]{1,0:T(8,128)(2,1)} fusion(f32[512,3328]{1,0:T(8,128)} %all-gather.6.cloned.1.call-done, bf16[256,3328]{1,0:T(8,128)(2,1)} %param.3, f32[128,256]{0,1:T(8,128)S(1)} %copy.44, f32[128,256]{0,1:T(8,128)S(1)} %copy.43, f32[128,256]{0,1:T(8,128)S(1)} %copy.42, f32[128,256]{0,1:T(8,128)S(1)} %fusion.53), kind=kOutput, calls=%fused_computation.4 | convolution fusion | flops 5237440512 | bytes 10747904 | tf_op jit(solution)/shard_map/dot_general | solution.py:81
  (80 shorter events, 21.4 us)
Async XLA Ops:
  7.2 65.7 %copy-start.1 = (bf16[256,3328]{1,0:T(8,128)(2,1)S(1)}, bf16[256,3328]{1,0:T(8,128)(2,1)}, u32[]{:S(2)}) copy-start(bf16[256,3328]{1,0:T(8,128)(2,1)} %param.3) | copy-start | bytes 5111812
  15.8 15.6 %all-to-all-start = ((f32[16,16,96]{2,1,0:T(8,128)}), f32[16,16,96]{2,1,0:T(8,128)S(1)}, u32[]{:S(2)}, u32[]{:S(2)}) async-start(f32[16,16,96]{2,1,0:T(8,128)} %broadcast_in_dim.56), calls=%async_computation | async-start | bytes 262144 | tf_op jit(solution)/shard_map/all_to_all | solution.py:12
  24.9 66.7 %all-gather.4.cloned.1.call-start = ((), (), s32[]{:S(2)}) async-start(), calls=%async_computation.2 | async-start | bytes 1572864 | tf_op jit(solution)/shard_map/all_gather | solution.py:31
  72.1 159.9 %all-gather.6.cloned.1.call-start = ((), (), s32[]{:S(2)}) async-start(), calls=%async_computation.3 | async-start | bytes 7028736 | tf_op jit(solution)/shard_map/all_gather | solution.py:83
  74.5 15.2 %all-to-all-start.1 = ((bf16[16,256,96]{1,2,0:T(8,128)(2,1)}), bf16[16,256,96]{1,2,0:T(8,128)(2,1)S(1)}, u32[]{:S(2)}, u32[]{:S(2)}) async-start(bf16[16,256,96]{1,2,0:T(8,128)(2,1)} %broadcast_in_dim.58), calls=%async_computation.1 | async-start | bytes 1572864 | tf_op jit(solution)/shard_map/all_to_all | solution.py:12
  115.3 110.2 %copy-start = (f32[256,512]{1,0:T(8,128)S(1)}, f32[256,512]{1,0:T(8,128)}, u32[]{:S(2)}) copy-start(f32[256,512]{1,0:T(8,128)} %fusion.2) | copy-start | bytes 1572868
Sparse Core Ops, SparseCore 0:
  72.2 12.8 all-gather.3
  87.2 78.6 all-gather.5
where the time goes:
time: 254 us; the launch traced here: 250 us
  other arithmetic  123 us (48%)
  blocking collectives  39.3 us (15%)
  matrix products  22.5 us (9%)
  between operations  19.2 us (8%)
  waiting for transfers between devices  16.5 us (6%)
  local copies, waits for them, and re-layouts  15.4 us (6%)
  starting transfers between devices  14.7 us (6%)
    another operation x15, other arithmetic, body(): factor_low = jnp.linalg.cholesky(schur_block)  79.5 us
    another operation x3, other arithmetic, body(): solved = jax.scipy.linalg.cho_solve((factor_low, True), weight_pruned.T).T  39.4 us
    all_gather x1, blocking collectives, all_blocks(): parts = lax.all_gather(parts, axes[k], axis=0, tiled=True)  39.3 us
    all_to_all x2, waiting for transfers between devices, from_everyone(): lax.all_to_all(jnp.broadcast_to(value[None], (count, *value.shape)), axis...  15.8 us
    all_to_all x2, starting transfers between devices, from_everyone(): lax.all_to_all(jnp.broadcast_to(value[None], (count, *value.shape)), axis...  14.6 us
    dot_general x1, matrix products, body(): jnp.dot(solved, lax.all_gather(inverse_rows, ROW, axis=0, tiled=True), pr...  11.3 us
    another operation x12, local copies, waits for them, and re-layouts  8.07 us
    another operation x14, matrix products, body(): solved = jax.scipy.linalg.cho_solve((factor_low, True), weight_pruned.T).T  5.41 us
  transfers between devices with their start and end apart: 4, of which 2 were waited for; matrix products, arithmetic and copies ran while one was open for 56% of the time, Pallas kernels for 0%

commit v1 on v0

--- a/solution.py
+++ b/solution.py
@@ -28,7 +28,9 @@
 def all_blocks(value, axes, sequence):
     parts = value[None]
     for k in sequence:
-        parts = lax.all_gather(parts, axes[k], axis=0, tiled=True)
+        parts = jnp.concatenate(
+            lax.all_to_all(jnp.stack([parts] * lax.axis_size(axes[k])), axes[k], 0, 0), axis=0
+        )
     carried = [lax.axis_size(axes[k]) for k in reversed(sequence)]
     parts = parts.reshape(*carried, *value.shape)
     turned = sorted(range(len(sequence)), key=lambda place: sequence[len(sequence) - 1 - place])

time: 254 us -> 266 us (1.047)
  the two profiles are of different devices: /device:TPU:8 before, /device:TPU:1 now
where the time goes in v1:
time: 266 us; the launch traced here: 262 us
  other arithmetic  123 us (46%)
  waiting for transfers between devices  40.4 us (15%)
  starting transfers between devices  28.3 us (11%)
  matrix products  23.9 us (9%)
  between operations  19.3 us (7%)
  local copies, waits for them, and re-layouts  15.1 us (6%)
  blocking collectives  12.2 us (5%)
    another operation x15, other arithmetic, body(): factor_low = jnp.linalg.cholesky(schur_block)  79.4 us
    another operation x3, other arithmetic, body(): solved = jax.scipy.linalg.cho_solve((factor_low, True), weight_pruned.T).T  39.6 us
    all_to_all x1, waiting for transfers between devices, all_blocks(): lax.all_to_all(jnp.stack([parts] * lax.axis_size(axes[k])), axes[k], 0, 0)  26.5 us
    all_to_all x1, starting transfers between devices, all_blocks(): lax.all_to_all(jnp.stack([parts] * lax.axis_size(axes[k])), axes[k], 0, 0)  17 us
    all_to_all x2, waiting for transfers between devices, from_everyone(): lax.all_to_all(jnp.broadcast_to(value[None], (count, *value.shape)), axis...  13.3 us
    all_to_all x1, blocking collectives, all_blocks(): lax.all_to_all(jnp.stack([parts] * lax.axis_size(axes[k])), axes[k], 0, 0)  12.2 us
    dot_general x1, matrix products, body(): jnp.dot(solved, lax.all_gather(inverse_rows, ROW, axis=0, tiled=True), pr...  11.3 us
    all_to_all x2, starting transfers between devices, from_everyone(): lax.all_to_all(jnp.broadcast_to(value[None], (count, *value.shape)), axis...  11.2 us
  transfers between devices with their start and end apart: 4, of which 3 were waited for; matrix products, arithmetic and copies ran while one was open for 57% of the time, Pallas kernels for 0%

profile of v1, /device:TPU:1, one launch (start us, length us, event | category | flops | bytes accessed | tf_op | source)
XLA Modules:
  0.0 261.9 jit_solution(12970037116085740567)
XLA Ops:
  7.9 1.4 copy.33
  13.5 1.5 compare_and_fusion
  16.4 7.6 %all-to-all-start = ((f32[16,16,96]{2,1,0:T(8,128)}), f32[16,16,96]{2,1,0:T(8,128)S(1)}, u32[]{:S(2)}, u32[]{:S(2)}) async-start(f32[16,16,96]{2,1,0:T(8,128)} %broadcast_in_dim.53), calls=%async_computation | async-start | bytes 262144 | tf_op jit(solution)/shard_map/all_to_all | solution.py:12
  24.0 2.1 fusion.12
  26.2 4.5 %all-to-all-done = f32[16,16,96]{2,1,0:T(8,128)S(1)} async-done(((f32[16,16,96]{2,1,0:T(8,128)}), f32[16,16,96]{2,1,0:T(8,128)S(1)}, u32[]{:S(2)}, u32[]{:S(2)}) %all-to-all-start) | async-done | bytes 98336 | tf_op jit(solution)/shard_map/all_to_all | solution.py:12
  31.7 3.6 %all-to-all-start.3 = ((bf16[16,256,96]{1,2,0:T(8,128)(2,1)}), bf16[16,256,96]{1,2,0:T(8,128)(2,1)S(1)}, u32[]{:S(2)}, u32[]{:S(2)}) async-start(bf16[16,256,96]{1,2,0:T(8,128)(2,1)} %broadcast_in_dim.54), calls=%async_computation.3 | async-start | bytes 1572864 | tf_op jit(solution)/shard_map/all_to_all | solution.py:12
  37.0 8.7 %all-to-all-done.3 = bf16[16,256,96]{1,2,0:T(8,128)(2,1)S(1)} async-done(((bf16[16,256,96]{1,2,0:T(8,128)(2,1)}), bf16[16,256,96]{1,2,0:T(8,128)(2,1)S(1)}, u32[]{:S(2)}, u32[]{:S(2)}) %all-to-all-start.3) | async-done | bytes 786464 | tf_op jit(solution)/shard_map/all_to_all | solution.py:12
  46.6 17.0 %all-to-all-start.1 = ((f32[16,1,16,512]{3,2,1,0:T(8,128)}), f32[16,1,16,512]{3,2,1,0:T(8,128)S(1)}, u32[]{:S(2)}, u32[]{:S(2)}) async-start(f32[16,1,16,512]{3,2,1,0:T(8,128)} %stack.6), calls=%async_computation.1 | async-start | bytes 1048576 | tf_op jit(solution)/shard_map/all_to_all | solution.py:32
  63.7 2.0 fusion.2
  65.7 26.5 %all-to-all-done.1 = f32[16,1,16,512]{3,2,1,0:T(8,128)S(1)} async-done(((f32[16,1,16,512]{3,2,1,0:T(8,128)}), f32[16,1,16,512]{3,2,1,0:T(8,128)S(1)}, u32[]{:S(2)}, u32[]{:S(2)}) %all-to-all-start.1) | async-done | bytes 524320 | tf_op jit(solution)/shard_map/all_to_all | solution.py:32
  92.3 12.2 %all_to_all.20 = f32[2,16,16,512]{3,2,1,0:T(8,128)S(1)} all-to-all(f32[2,16,16,512]{3,2,1,0:T(8,128)S(1)} %pad_maximum_fusion), channel_id=1, replica_groups=mesh['row_0'=16,'row_1'=2,'col'=16] {'row_1'}, dimensions={0} | all-to-all | bytes 2097152 | tf_op jit(solution)/shard_map/all_to_all | solution.py:32
  105.1 11.7 %cholesky.104 = f32[128,128]{1,0:T(8,128)S(1)} custom-call(f32[128,128]{1,0:T(8,128)S(1)} %cholesky.266), custom_call_target="Cholesky" | custom-call | tf_op jit(solution)/shard_map/jit(cholesky)/cholesky | solution.py:81
  117.0 9.8 %custom-call.34 = f32[1,128,128]{1,2,0:T(8,128)S(1)} custom-call(f32[1,128,128]{2,1,0:T(8,128)S(1)} %get-tuple-element.31), custom_call_target="InvertDiagBlocksLowerTriangular" | custom-call | tf_op jit(solution)/shard_map/jit(cholesky)/cholesky | solution.py:81
  127.5 11.7 %cholesky.217 = f32[128,128]{1,0:T(8,128)S(1)} custom-call(f32[128,128]{1,0:T(8,128)S(1)} %cholesky.270), custom_call_target="Cholesky" | custom-call | tf_op jit(solution)/shard_map/jit(cholesky)/cholesky | solution.py:81
  139.2 10.0 %custom-call.35 = f32[1,128,128]{1,2,0:T(8,128)S(1)} custom-call(f32[1,128,128]{2,1,0:T(8,128)S(1)} %get-tuple-element.28), custom_call_target="InvertDiagBlocksLowerTriangular" | custom-call | tf_op jit(solution)/shard_map/jit(cholesky)/cholesky | solution.py:81
  149.9 11.7 %cholesky.238 = f32[128,128]{1,0:T(8,128)S(1)} custom-call(f32[128,128]{1,0:T(8,128)S(1)} %cholesky.275), custom_call_target="Cholesky" | custom-call | tf_op jit(solution)/shard_map/jit(cholesky)/cholesky | solution.py:81
  161.6 9.8 %custom-call.36 = f32[1,128,128]{1,2,0:T(8,128)S(1)} custom-call(f32[1,128,128]{2,1,0:T(8,128)S(1)} %get-tuple-element.25), custom_call_target="InvertDiagBlocksLowerTriangular" | custom-call | tf_op jit(solution)/shard_map/jit(cholesky)/cholesky | solution.py:81
  172.0 11.7 %cholesky.255 = f32[128,128]{1,0:T(8,128)S(1)} custom-call(f32[128,128]{1,0:T(8,128)S(1)} %convolution_subtract_fusion.9), custom_call_target="Cholesky" | custom-call | tf_op jit(solution)/shard_map/jit(cholesky)/cholesky | solution.py:81
  189.6 8.2 %while.1 = (s32[]{:T(128)}, f32[512,512]{1,0:T(8,128)S(1)}, s32[4,2]{0,1:T(2,128)S(1)}, f32[4,128,128]{2,1,0:T(8,128)S(1)}, s32[]{:T(128)}) while((s32[]{:T(128)}, f32[512,512]{1,0:T(8,128)S(1)}, s32[4,2]{0,1:T(2,128)S(1)}, f32[4,128,128]{2,1,0:T(8,128)S(1)}, s32[]{:T(128)}) %tuple.33), condition=%wide.while_cond, body=%wide.while_body.sunk | while | flops 2 | bytes 131181 | solution.py:82
  190.2 1.3 bitcast_dynamic-update-slice_fusion.2
  192.3 1.3 bitcast_dynamic-update-slice_fusion.2
  194.3 1.3 bitcast_dynamic-update-slice_fusion.2
  197.7 39.3 %custom-call.37 = f32[4,128,128]{1,2,0:T(8,128)S(1)} custom-call(f32[4,128,128]{2,1,0:T(8,128)S(1)} %get-tuple-element.9), custom_call_target="InvertDiagBlocksLowerTriangular" | custom-call | tf_op jit(solution)/shard_map/jit(_cho_solve)/triangular_solve | solution.py:82
  243.6 11.3 %fusion = bf16[256,3328]{1,0:T(8,128)(2,1)} fusion(f32[512,3328]{1,0:T(8,128)} %all-gather.2.cloned.1.call-done, bf16[256,3328]{1,0:T(8,128)(2,1)} %param.3, f32[128,256]{0,1:T(8,128)S(1)} %copy.44, f32[128,256]{0,1:T(8,128)S(1)} %copy.43, f32[128,256]{0,1:T(8,128)S(1)} %copy.42, f32[128,256]{0,1:T(8,128)S(1)} %fusion.53), kind=kOutput, calls=%fused_computation.4 | convolution fusion | flops 5237440512 | bytes 10747904 | tf_op jit(solution)/shard_map/dot_general | solution.py:83
  (79 shorter events, 24.4 us)
Async XLA Ops:
  7.2 236.4 %all-gather.2.cloned.1.call-start = ((), (), s32[]{:S(2)}) async-start(), calls=%async_computation.4 | async-start | bytes 7028736 | tf_op jit(solution)/shard_map/all_gather | solution.py:85
  16.4 14.3 %all-to-all-start = ((f32[16,16,96]{2,1,0:T(8,128)}), f32[16,16,96]{2,1,0:T(8,128)S(1)}, u32[]{:S(2)}, u32[]{:S(2)}) async-start(f32[16,16,96]{2,1,0:T(8,128)} %broadcast_in_dim.53), calls=%async_computation | async-start | bytes 262144 | tf_op jit(solution)/shard_map/all_to_all | solution.py:12
  31.7 14.0 %all-to-all-start.3 = ((bf16[16,256,96]{1,2,0:T(8,128)(2,1)}), bf16[16,256,96]{1,2,0:T(8,128)(2,1)S(1)}, u32[]{:S(2)}, u32[]{:S(2)}) async-start(bf16[16,256,96]{1,2,0:T(8,128)(2,1)} %broadcast_in_dim.54), calls=%async_computation.3 | async-start | bytes 1572864 | tf_op jit(solution)/shard_map/all_to_all | solution.py:12
  46.6 45.5 %all-to-all-start.1 = ((f32[16,1,16,512]{3,2,1,0:T(8,128)}), f32[16,1,16,512]{3,2,1,0:T(8,128)S(1)}, u32[]{:S(2)}, u32[]{:S(2)}) async-start(f32[16,1,16,512]{3,2,1,0:T(8,128)} %stack.6), calls=%async_computation.1 | async-start | bytes 1048576 | tf_op jit(solution)/shard_map/all_to_all | solution.py:32
  126.8 110.2 %copy-start = (f32[256,512]{1,0:T(8,128)S(1)}, f32[256,512]{1,0:T(8,128)}, u32[]{:S(2)}) copy-start(f32[256,512]{1,0:T(8,128)} %fusion.2) | copy-start | bytes 1572868
Sparse Core Ops, SparseCore 0:
  10.1 101.8 all-gather.1
